TPU v7x, 256 devices: a whole 4x4x8 slice. The times are simulated.
256 devices in a mesh: loop: 16 (over z, y_lo), rep: 16 (over y_hi, x, core).
Axes of the slice: x: 4, y: 4 (y_hi: 2, y_lo: 2; y = y_hi * 2 + y_lo), z: 8, core: 2. Of those that a mesh axis runs over, the one named last changes fastest.
Arguments:
- features: bfloat16 [65536, 128], P(('loop', 'rep')), may hold values from -6 to 6
- w_self: bfloat16 [128, 256], replicated, may hold values from -0.5 to 0.5
- w_neigh: bfloat16 [128, 256], replicated, may hold values from -0.5 to 0.5
- bias: float32 [256], replicated, may hold values from -3 to 3
- degree: int32 [65536], P(('loop', 'rep')), may hold values from 1 to 4
- tiles: bfloat16 [16, 16, 16, 16, 128, 128], P('loop', 'rep'), may hold values from -0.0625 to 0.0625
- dst_block: int32 [16, 16, 16, 16], P('loop', 'rep'), may hold values from 0 to 31, as said below
- src_block: int32 [16, 16, 16, 16], P('loop', 'rep'), may hold values from 0 to 1, as said below
- live_count: int32 [16, 16, 16], P('loop', 'rep'), may hold values from 1 to 16, as said below
- cotangent: bfloat16 [65536, 256], P(('loop', 'rep')), may hold values from -6 to 6
Outputs:
- output: bfloat16 [65536, 256], P(('loop', 'rep'))
- grad_input: bfloat16 [65536, 128], P(('loop', 'rep'))
- grad_self: float32 [128, 256], replicated
- grad_neigh: float32 [128, 256], replicated
- grad_bias: float32 [256], replicated
Inputs may be any that keep to these rules, and one draw needn't show every extreme that they name: Within one (p, r, q) the 16 slots name distinct pairs (dst_block, src_block). Within one (p, r, q) the 16 slots name distinct pairs (dst_block, src_block). `live_count`: every device (p, r) has some q with all 16 slots live; slots at or past the count hold tiles that are not part of the graph.
All inputs are finite; a program needn't handle non-finite values.
Results may differ from a plain program's by a relative error of at most 0.0075.
Values may be sent and summed in bfloat16 or wider, within the bound.
A program may use at most 128 MiB of HBM per device.

v0:
```python
import math
import jax
import jax.numpy as jnp
from jax import lax
from jax.sharding import PartitionSpec as P


def shifted(block, axis, distance):
    devices = range(lax.axis_size(axis))
    route = [((i - distance) % len(devices), i) for i in devices]
    return lax.ppermute(block, axis, route)


def per_device(
    features, w_self, w_neigh, bias, degree, tiles, dst_block, src_block, live_count, cotangent
):
    loop_count = lax.axis_size("loop")
    rep_count = lax.axis_size("rep")
    loop_here = lax.axis_index("loop")
    row_count, feat_width = features.shape
    tile_size = tiles.shape[-1]
    slot_count = tiles.shape[3]
    sub_blocks = row_count // tile_size
    row_blocks = sub_blocks * rep_count
    tile_all = tiles[0, 0]
    dst_all = dst_block[0, 0]
    src_all = src_block[0, 0]
    live_all = jnp.arange(slot_count)[None, :] < live_count[0, 0][:, None]
    place_all = (
        (dst_all[:, :, None] == jnp.arange(row_blocks)[None, None, :]) & live_all[:, :, None]
    ).astype(jnp.float32)
    land_all = (
        (src_all[:, :, None] == jnp.arange(sub_blocks)[None, None, :]) & live_all[:, :, None]
    ).astype(jnp.float32)

    def pick_entry(table, source):
        return lax.dynamic_index_in_dim(table, source, 0, keepdims=False)

    def gather_term(source, panel):
        tile_part = pick_entry(tile_all, source)
        chosen = jnp.take(
            panel.reshape(sub_blocks, tile_size, feat_width), pick_entry(src_all, source), axis=0
        )
        product = jnp.einsum("tij,tjf->tif", tile_part, chosen, preferred_element_type=jnp.float32)
        return jnp.einsum(
            "td,tif->dif", pick_entry(place_all, source), product, precision=lax.Precision.HIGHEST
        )

    running = gather_term(loop_here, features)

    def one_way(step_index, state):
        panel, total = state
        panel = shifted(panel, "loop", 1)
        return (panel, total + gather_term((loop_here - step_index) % loop_count, panel))

    _, running = lax.fori_loop(1, loop_count, one_way, (features, running))
    agg_sum = lax.psum_scatter(
        running.reshape(row_blocks * tile_size, feat_width), "rep", scatter_dimension=0, tiled=True
    )
    degree_f = degree.astype(jnp.float32)[:, None]
    aggregate = (agg_sum / degree_f).astype(jnp.bfloat16)
    preact = (
        jnp.dot(features, w_self, preferred_element_type=jnp.float32)
        + jnp.dot(aggregate, w_neigh, preferred_element_type=jnp.float32)
        + bias
    )
    sigmoid_val = jax.nn.sigmoid(preact)
    output = (preact * sigmoid_val).astype(jnp.bfloat16)
    grad_pre = (
        cotangent.astype(jnp.float32) * sigmoid_val * (1.0 + preact * (1.0 - sigmoid_val))
    ).astype(jnp.bfloat16)
    grad_agg = (
        jnp.einsum("nh,fh->nf", grad_pre, w_neigh, preferred_element_type=jnp.float32) / degree_f
    ).astype(jnp.bfloat16)
    grad_whole = lax.all_gather(grad_agg, "rep", axis=0, tiled=True).reshape(
        row_blocks, tile_size, feat_width
    )
    node_total = row_count * loop_count * rep_count
    grad_scale = 1.0 / math.sqrt(node_total)
    grad_self, grad_neigh, grad_bias = lax.psum(
        (
            jnp.einsum("nf,nh->fh", features, grad_pre, preferred_element_type=jnp.float32)
            * grad_scale,
            jnp.einsum("nf,nh->fh", aggregate, grad_pre, preferred_element_type=jnp.float32)
            * grad_scale,
            jnp.sum(grad_pre.astype(jnp.float32), axis=0) * grad_scale,
        ),
        ("loop", "rep"),
    )
    self_grad = jnp.einsum("nh,fh->nf", grad_pre, w_self, preferred_element_type=jnp.float32)

    def spread_term(source):
        tile_part = pick_entry(tile_all, source)
        chosen = jnp.take(grad_whole, pick_entry(dst_all, source), axis=0)
        product = jnp.einsum("tij,tif->tjf", tile_part, chosen, preferred_element_type=jnp.float32)
        summed = jnp.einsum(
            "ts,tjf->sjf", pick_entry(land_all, source), product, precision=lax.Precision.HIGHEST
        )
        return summed.reshape(row_count, feat_width)

    def carry_along(step_index, total):
        total = shifted(total, "loop", -1)
        return total + spread_term((loop_here + 1 + step_index) % loop_count)

    neigh_grad = lax.fori_loop(
        1, loop_count, carry_along, spread_term((loop_here + 1) % loop_count)
    )
    grad_input = (self_grad + neigh_grad).astype(jnp.bfloat16)
    return (output, grad_input, grad_self, grad_neigh, grad_bias)


def solution(mesh):
    in_specs = (
        P(("loop", "rep"), None),
        P(),
        P(),
        P(),
        P(("loop", "rep")),
        P("loop", "rep", None, None, None, None),
        P("loop", "rep", None, None),
        P("loop", "rep", None, None),
        P("loop", "rep", None),
        P(("loop", "rep"), None),
    )
    out_specs = (P(("loop", "rep"), None), P(("loop", "rep"), None), P(), P(), P())
    return jax.shard_map(
        per_device, mesh=mesh, in_specs=in_specs, out_specs=out_specs, check_vma=False
    )
```

profile of v0, /device:TPU:2, one launch (start us, length us, event | category | flops | bytes accessed | tf_op | source)
XLA Modules:
  0.0 704.0 jit_solution(3189512164626604518)
XLA Ops:
  14.8 174.0 %while.32 = (s32[]{:T(128)}, bf16[256,128]{1,0:T(8,128)(2,1)S(1)}, f32[32,128,128]{2,0,1:T(8,128)S(1)}, s32[]{:T(128)}, f32[16,16,32]{2,1,0:T(8,128)S(1)}, /*ind...) while((s32[]{:T(128)}, bf16[256,128]{1,0:T(8,128)(2,1)S(1)}, ...), condition=%wide.region_1.3_spmd, body=%wide.region_0.2_spmd.sunk | while | flops 168559728 | bytes 8794716 | solution.py:56
  16.5 7.5 %collective-permute-done = bf16[256,128]{1,0:T(8,128)(2,1)S(1)} collective-permute-done((bf16[256,128]{1,0:T(8,128)(2,1)S(1)}, bf16[256,128]{1,0:T(8,128)(2,1)S(1)}, u32[]{:S(2)}, u32[]{:S(2)}) %collective-permute-start) | collective-permute-done | bytes 65568 | tf_op jit(solution)/shard_map/while/body/eval_jaxpr/ppermute | solution.py:11
  29.1 6.3 collective-permute-done
  40.5 6.3 collective-permute-done
  51.8 6.3 collective-permute-done
  63.2 6.3 collective-permute-done
  74.6 6.3 collective-permute-done
  86.0 6.3 collective-permute-done
  97.4 6.3 collective-permute-done
  108.8 6.8 collective-permute-done
  120.7 6.3 collective-permute-done
  132.0 6.3 collective-permute-done
  143.4 6.3 collective-permute-done
  154.8 6.3 collective-permute-done
  166.2 6.3 collective-permute-done
  177.6 6.3 collective-permute-done
  192.4 77.7 %reduce-scatter.2.cloned.1.call-done = f32[256,128]{1,0:T(8,128)} async-done(((f32[4096,128]{1,0:T(8,128)}), f32[256,128]{1,0:T(8,128)}) %reduce-scatter.2.cloned.1.call-update) | async-done | bytes 131088 | tf_op jit(solution)/shard_map/reduce_scatter | solution.py:57
  275.6 74.1 %psum.23 = f32[256]{0:T(256)} all-reduce(f32[256]{0:T(256)S(1)} %broadcast_multiply_fusion), channel_id=1, replica_groups=mesh['loop'=16,'rep'=16] {'loop','rep'}, use_global_device_ids=true, to_apply=%region_8.11 | all-reduce | flops 256 | bytes 2048 | tf_op jit(solution)/shard_map/psum | solution.py:80
  349.7 177.0 %all-reduce.3.cloned.1.call-done = (f32[128,256]{0,1:T(8,128)}, f32[128,256]{1,0:T(8,128)}) async-done(((f32[128,256]{0,1:T(8,128)}, f32[128,256]{1,0:T(8,128)}), (f32[128,256]{0,1:T(8,128)}, f32[128,256]{1,0:T(8,128)})) %all-reduce.3.cloned.1.call-update) | async-done | bytes 262160 | tf_op jit(solution)/shard_map/psum | solution.py:80
  528.4 50.3 %all-gather.2.cloned.1.call-done = bf16[4096,128]{1,0:T(8,128)(2,1)} async-done(((bf16[256,128]{1,0:T(8,128)(2,1)}), bf16[4096,128]{1,0:T(8,128)(2,1)}) %all-gather.2.cloned.1.call-update) | async-done | bytes 1048592 | tf_op jit(solution)/shard_map/all_gather | solution.py:75
  583.2 112.8 %while.33 = (s32[]{:T(128)}, f32[256,128]{1,0:T(8,128)S(1)}, s32[]{:T(128)}, f32[16,16,2]{1,2,0:T(2,128)S(1)}, bf16[16,16,128,128]{3,2,1,0:T(8,128)(2,1)}, /*ind...) while((s32[]{:T(128)}, f32[256,128]{1,0:T(8,128)S(1)}, ...), condition=%wide.region_4.7_spmd, body=%wide.region_3.6_spmd.sunk | while | flops 73696368 | bytes 5510748 | solution.py:105
  583.2 3.4 collective-permute-start.1
  590.6 3.8 collective-permute-start.1
  598.5 3.1 collective-permute-start.1
  605.7 3.1 collective-permute-start.1
  620.1 3.5 collective-permute-start.1
  627.6 4.5 collective-permute-start.1
  636.1 3.6 collective-permute-start.1
  650.9 3.1 collective-permute-start.1
  665.3 3.8 collective-permute-start.1
  673.1 4.2 collective-permute-start.1
  681.3 3.4 collective-permute-start.1
  (281 shorter events, 173.0 us)
Async XLA Ops:
  7.2 262.9 %reduce-scatter.2.cloned.1.call-start = ((), (), s32[]{:S(2)}) async-start(), calls=%async_computation.1 | async-start | bytes 2228224 | tf_op jit(solution)/shard_map/reduce_scatter | solution.py:57
  14.8 9.2 %collective-permute-start = (bf16[256,128]{1,0:T(8,128)(2,1)S(1)}, bf16[256,128]{1,0:T(8,128)(2,1)S(1)}, u32[]{:S(2)}, u32[]{:S(2)}) collective-permute-start(bf16[256,128]{1,0:T(8,128)(2,1)S(1)} %get-tuple-element.526), channel_id=1, source_target_pairs={{240,0},{0,16},{16,32},{32,48},{48,64},{64,80},{80,96},{96,112},{1... | collective-permute-start | bytes 196616 | tf_op jit(solution)/shard_map/while/body/eval_jaxpr/ppermute | solution.py:11
  28.9 6.5 collective-permute-start
  40.3 6.5 collective-permute-start
  51.7 6.5 collective-permute-start
  63.1 6.5 collective-permute-start
  74.5 6.5 collective-permute-start
  85.8 6.5 collective-permute-start
  97.2 6.5 collective-permute-start
  108.6 7.0 collective-permute-start
  120.5 6.5 collective-permute-start
  143.3 6.5 collective-permute-start
  154.7 6.5 collective-permute-start
  166.1 6.5 collective-permute-start
  177.4 6.5 collective-permute-start
  191.4 335.3 %all-reduce.3.cloned.1.call-start = ((), (), s32[]{:S(2)}) async-start(), calls=%async_computation.3 | async-start | bytes 524288 | tf_op jit(solution)/shard_map/psum | solution.py:80
  273.9 304.7 %all-gather.2.cloned.1.call-start = ((), (), s32[]{:S(2)}) async-start(), calls=%async_computation.2 | async-start | bytes 1114112 | tf_op jit(solution)/shard_map/all_gather | solution.py:75
  583.2 7.4 %collective-permute-start.1 = (f32[256,128]{1,0:T(8,128)S(1)}, f32[256,128]{1,0:T(8,128)S(1)}, u32[]{:S(2)}, u32[]{:S(2)}) collective-permute-start(f32[256,128]{1,0:T(8,128)S(1)} %get-tuple-element.559), channel_id=1, source_target_pairs={{16,0},{32,16},{48,32},{64,48},{80,64},{96,80},{112,96},{128,112},... | collective-permute-start | bytes 393224 | tf_op jit(solution)/shard_map/while/body/eval_jaxpr/ppermute | solution.py:11
  590.6 7.8 %collective-permute-start.1 = (f32[256,128]{1,0:T(8,128)S(1)}, f32[256,128]{1,0:T(8,128)S(1)}, u32[]{:S(2)}, u32[]{:S(2)}) collective-permute-start(f32[256,128]{1,0:T(8,128)S(1)} %get-tuple-element.559), channel_id=1, source_target_pairs={{16,0},{32,16},{48,32},{64,48},{80,64},{96,80},{112,96},{128,112},... | collective-permute-start | bytes 393224 | tf_op jit(solution)/shard_map/while/body/eval_jaxpr/ppermute | solution.py:11
  598.5 7.1 %collective-permute-start.1 = (f32[256,128]{1,0:T(8,128)S(1)}, f32[256,128]{1,0:T(8,128)S(1)}, u32[]{:S(2)}, u32[]{:S(2)}) collective-permute-start(f32[256,128]{1,0:T(8,128)S(1)} %get-tuple-element.559), channel_id=1, source_target_pairs={{16,0},{32,16},{48,32},{64,48},{80,64},{96,80},{112,96},{128,112},... | collective-permute-start | bytes 393224 | tf_op jit(solution)/shard_map/while/body/eval_jaxpr/ppermute | solution.py:11
  605.7 7.1 %collective-permute-start.1 = (f32[256,128]{1,0:T(8,128)S(1)}, f32[256,128]{1,0:T(8,128)S(1)}, u32[]{:S(2)}, u32[]{:S(2)}) collective-permute-start(f32[256,128]{1,0:T(8,128)S(1)} %get-tuple-element.559), channel_id=1, source_target_pairs={{16,0},{32,16},{48,32},{64,48},{80,64},{96,80},{112,96},{128,112},... | collective-permute-start | bytes 393224 | tf_op jit(solution)/shard_map/while/body/eval_jaxpr/ppermute | solution.py:11
  612.9 7.1 %collective-permute-start.1 = (f32[256,128]{1,0:T(8,128)S(1)}, f32[256,128]{1,0:T(8,128)S(1)}, u32[]{:S(2)}, u32[]{:S(2)}) collective-permute-start(f32[256,128]{1,0:T(8,128)S(1)} %get-tuple-element.559), channel_id=1, source_target_pairs={{16,0},{32,16},{48,32},{64,48},{80,64},{96,80},{112,96},{128,112},... | collective-permute-start | bytes 393224 | tf_op jit(solution)/shard_map/while/body/eval_jaxpr/ppermute | solution.py:11
  620.1 7.5 %collective-permute-start.1 = (f32[256,128]{1,0:T(8,128)S(1)}, f32[256,128]{1,0:T(8,128)S(1)}, u32[]{:S(2)}, u32[]{:S(2)}) collective-permute-start(f32[256,128]{1,0:T(8,128)S(1)} %get-tuple-element.559), channel_id=1, source_target_pairs={{16,0},{32,16},{48,32},{64,48},{80,64},{96,80},{112,96},{128,112},... | collective-permute-start | bytes 393224 | tf_op jit(solution)/shard_map/while/body/eval_jaxpr/ppermute | solution.py:11
  627.6 8.5 %collective-permute-start.1 = (f32[256,128]{1,0:T(8,128)S(1)}, f32[256,128]{1,0:T(8,128)S(1)}, u32[]{:S(2)}, u32[]{:S(2)}) collective-permute-start(f32[256,128]{1,0:T(8,128)S(1)} %get-tuple-element.559), channel_id=1, source_target_pairs={{16,0},{32,16},{48,32},{64,48},{80,64},{96,80},{112,96},{128,112},... | collective-permute-start | bytes 393224 | tf_op jit(solution)/shard_map/while/body/eval_jaxpr/ppermute | solution.py:11
  636.1 7.6 %collective-permute-start.1 = (f32[256,128]{1,0:T(8,128)S(1)}, f32[256,128]{1,0:T(8,128)S(1)}, u32[]{:S(2)}, u32[]{:S(2)}) collective-permute-start(f32[256,128]{1,0:T(8,128)S(1)} %get-tuple-element.559), channel_id=1, source_target_pairs={{16,0},{32,16},{48,32},{64,48},{80,64},{96,80},{112,96},{128,112},... | collective-permute-start | bytes 393224 | tf_op jit(solution)/shard_map/while/body/eval_jaxpr/ppermute | solution.py:11
  643.7 7.1 %collective-permute-start.1 = (f32[256,128]{1,0:T(8,128)S(1)}, f32[256,128]{1,0:T(8,128)S(1)}, u32[]{:S(2)}, u32[]{:S(2)}) collective-permute-start(f32[256,128]{1,0:T(8,128)S(1)} %get-tuple-element.559), channel_id=1, source_target_pairs={{16,0},{32,16},{48,32},{64,48},{80,64},{96,80},{112,96},{128,112},... | collective-permute-start | bytes 393224 | tf_op jit(solution)/shard_map/while/body/eval_jaxpr/ppermute | solution.py:11
  650.9 7.1 %collective-permute-start.1 = (f32[256,128]{1,0:T(8,128)S(1)}, f32[256,128]{1,0:T(8,128)S(1)}, u32[]{:S(2)}, u32[]{:S(2)}) collective-permute-start(f32[256,128]{1,0:T(8,128)S(1)} %get-tuple-element.559), channel_id=1, source_target_pairs={{16,0},{32,16},{48,32},{64,48},{80,64},{96,80},{112,96},{128,112},... | collective-permute-start | bytes 393224 | tf_op jit(solution)/shard_map/while/body/eval_jaxpr/ppermute | solution.py:11
  658.1 7.1 %collective-permute-start.1 = (f32[256,128]{1,0:T(8,128)S(1)}, f32[256,128]{1,0:T(8,128)S(1)}, u32[]{:S(2)}, u32[]{:S(2)}) collective-permute-start(f32[256,128]{1,0:T(8,128)S(1)} %get-tuple-element.559), channel_id=1, source_target_pairs={{16,0},{32,16},{48,32},{64,48},{80,64},{96,80},{112,96},{128,112},... | collective-permute-start | bytes 393224 | tf_op jit(solution)/shard_map/while/body/eval_jaxpr/ppermute | solution.py:11
  665.3 7.8 %collective-permute-start.1 = (f32[256,128]{1,0:T(8,128)S(1)}, f32[256,128]{1,0:T(8,128)S(1)}, u32[]{:S(2)}, u32[]{:S(2)}) collective-permute-start(f32[256,128]{1,0:T(8,128)S(1)} %get-tuple-element.559), channel_id=1, source_target_pairs={{16,0},{32,16},{48,32},{64,48},{80,64},{96,80},{112,96},{128,112},... | collective-permute-start | bytes 393224 | tf_op jit(solution)/shard_map/while/body/eval_jaxpr/ppermute | solution.py:11
  673.1 8.2 %collective-permute-start.1 = (f32[256,128]{1,0:T(8,128)S(1)}, f32[256,128]{1,0:T(8,128)S(1)}, u32[]{:S(2)}, u32[]{:S(2)}) collective-permute-start(f32[256,128]{1,0:T(8,128)S(1)} %get-tuple-element.559), channel_id=1, source_target_pairs={{16,0},{32,16},{48,32},{64,48},{80,64},{96,80},{112,96},{128,112},... | collective-permute-start | bytes 393224 | tf_op jit(solution)/shard_map/while/body/eval_jaxpr/ppermute | solution.py:11
  681.3 7.4 %collective-permute-start.1 = (f32[256,128]{1,0:T(8,128)S(1)}, f32[256,128]{1,0:T(8,128)S(1)}, u32[]{:S(2)}, u32[]{:S(2)}) collective-permute-start(f32[256,128]{1,0:T(8,128)S(1)} %get-tuple-element.559), channel_id=1, source_target_pairs={{16,0},{32,16},{48,32},{64,48},{80,64},{96,80},{112,96},{128,112},... | collective-permute-start | bytes 393224 | tf_op jit(solution)/shard_map/while/body/eval_jaxpr/ppermute | solution.py:11
  688.8 7.1 %collective-permute-start.1 = (f32[256,128]{1,0:T(8,128)S(1)}, f32[256,128]{1,0:T(8,128)S(1)}, u32[]{:S(2)}, u32[]{:S(2)}) collective-permute-start(f32[256,128]{1,0:T(8,128)S(1)} %get-tuple-element.559), channel_id=1, source_target_pairs={{16,0},{32,16},{48,32},{64,48},{80,64},{96,80},{112,96},{128,112},... | collective-permute-start | bytes 393224 | tf_op jit(solution)/shard_map/while/body/eval_jaxpr/ppermute | solution.py:11
  (11 other events, 551.8 us)
Sparse Core Ops, SparseCore 0:
  191.5 78.5 reduce-scatter.1
  276.3 250.3 all-reduce.2
  530.0 48.5 all-gather.1
where the time goes:
time: 706 us; the launch traced here: 704 us
  waiting for transfers between devices  401 us (57%)
  matrix products  114 us (16%)
  blocking collectives  74.1 us (10%)
  starting transfers between devices  55.1 us (8%)
  local copies, waits for them, and re-layouts  29.7 us (4%)
  other arithmetic  14.1 us (2%)
  between operations  13.9 us (2%)
    psum x1, waiting for transfers between devices, per_device(): lax.psum((jnp.einsum('nf,nh->fh', features, grad_pre, preferred_element_t...  177 us
    ppermute x30, waiting for transfers between devices, shifted(): return lax.ppermute(block, axis, route)  96.3 us
    reduce_scatter x1, waiting for transfers between devices, per_device(): lax.psum_scatter(running.reshape(row_blocks * tile_size, feat_width), 're...  77.7 us
    psum x1, blocking collectives, per_device(): lax.psum((jnp.einsum('nf,nh->fh', features, grad_pre, preferred_element_t...  74.1 us
    ppermute x30, starting transfers between devices, shifted(): return lax.ppermute(block, axis, route)  55 us
    all_gather x1, waiting for transfers between devices, per_device(): lax.all_gather(grad_agg, 'rep', axis=0, tiled=True)  50.3 us
    dot_general x16, matrix products, gather_term(): jnp.einsum('td,tif->dif', pick_entry(place_all, source), product, precisi...  43.8 us
    dot_general x16, matrix products, spread_term(): jnp.einsum('tij,tif->tjf', tile_part, chosen, preferred_element_type=jnp....  22.8 us
  transfers between devices with their start and end apart: 33, of which 18 were waited for; matrix products, arithmetic and copies ran while one was open for 9% of the time, Pallas kernels for 0%

commit v1 on v0

--- a/solution.py
+++ b/solution.py
@@ -3,6 +3,11 @@
 import jax.numpy as jnp
 from jax import lax
 from jax.sharding import PartitionSpec as P
+
+
+def exchange_gather(x, name, along):
+    stack = jnp.stack([x] * lax.axis_size(name))
+    return jnp.concatenate(lax.all_to_all(stack, name, 0, 0), axis=along)
 
 
 def shifted(block, axis, distance):
@@ -72,9 +77,7 @@
     grad_agg = (
         jnp.einsum("nh,fh->nf", grad_pre, w_neigh, preferred_element_type=jnp.float32) / degree_f
     ).astype(jnp.bfloat16)
-    grad_whole = lax.all_gather(grad_agg, "rep", axis=0, tiled=True).reshape(
-        row_blocks, tile_size, feat_width
-    )
+    grad_whole = exchange_gather(grad_agg, "rep", 0).reshape(row_blocks, tile_size, feat_width)
     node_total = row_count * loop_count * rep_count
     grad_scale = 1.0 / math.sqrt(node_total)
     grad_self, grad_neigh, grad_bias = lax.psum(

time: 706 us -> 665 us (0.942)
  waiting for transfers between devices: 401 us -> 351 us
    all_gather x1 -> x0, waiting for transfers between devices: 50.3 us -> none  [per_device(): lax.all_gather(grad_agg, 'rep', axis=0, tiled=True)]
  transfers between devices with their start and end apart: 33 -> 33, of which waited for: 18 -> 17; matrix products, arithmetic and copies ran while one was open for 9% -> 10% of each run, Pallas kernels for 0% -> 0%
where the time goes in v1:
time: 665 us; the launch traced here: 663 us
  waiting for transfers between devices  351 us (53%)
  matrix products  113 us (17%)
  blocking collectives  80.1 us (12%)
  starting transfers between devices  59 us (9%)
  local copies, waits for them, and re-layouts  29.4 us (4%)
  other arithmetic  14.2 us (2%)
  between operations  14.2 us (2%)
    psum x1, waiting for transfers between devices, per_device(): lax.psum((jnp.einsum('nf,nh->fh', features, grad_pre, preferred_element_t...  177 us
    ppermute x30, waiting for transfers between devices, shifted(): return lax.ppermute(block, axis, route)  96.3 us
    psum x1, blocking collectives, per_device(): lax.psum((jnp.einsum('nf,nh->fh', features, grad_pre, preferred_element_t...  80.1 us
    reduce_scatter x1, waiting for transfers between devices, per_device(): lax.psum_scatter(running.reshape(row_blocks * tile_size, feat_width), 're...  77.2 us
    ppermute x30, starting transfers between devices, shifted(): return lax.ppermute(block, axis, route)  53.5 us
    dot_general x16, matrix products, gather_term(): jnp.einsum('td,tif->dif', pick_entry(place_all, source), product, precisi...  43.8 us
    dot_general x16, matrix products, spread_term(): jnp.einsum('tij,tif->tjf', tile_part, chosen, preferred_element_type=jnp....  22.8 us
    dot_general x16, matrix products, gather_term(): jnp.einsum('tij,tjf->tif', tile_part, chosen, preferred_element_type=jnp....  22.6 us
  transfers between devices with their start and end apart: 33, of which 17 were waited for; matrix products, arithmetic and copies ran while one was open for 10% of the time, Pallas kernels for 0%

profile of v1, /device:TPU:2, one launch (start us, length us, event | category | flops | bytes accessed | tf_op | source)
XLA Modules:
  0.0 662.6 jit_solution(9859981537833282876)
XLA Ops:
  14.8 174.0 %while.32 = (s32[]{:T(128)}, bf16[256,128]{1,0:T(8,128)(2,1)S(1)}, f32[32,128,128]{2,0,1:T(8,128)S(1)}, s32[]{:T(128)}, f32[16,16,32]{2,1,0:T(8,128)S(1)}, /*ind...) while((s32[]{:T(128)}, bf16[256,128]{1,0:T(8,128)(2,1)S(1)}, ...), condition=%wide.region_1.3_spmd, body=%wide.region_0.2_spmd.sunk | while | flops 168559728 | bytes 8794716 | solution.py:61
  16.5 7.5 %collective-permute-done = bf16[256,128]{1,0:T(8,128)(2,1)S(1)} collective-permute-done((bf16[256,128]{1,0:T(8,128)(2,1)S(1)}, bf16[256,128]{1,0:T(8,128)(2,1)S(1)}, u32[]{:S(2)}, u32[]{:S(2)}) %collective-permute-start) | collective-permute-done | bytes 65568 | tf_op jit(solution)/shard_map/while/body/eval_jaxpr/ppermute | solution.py:16
  29.1 6.3 collective-permute-done
  40.5 6.3 collective-permute-done
  51.9 6.3 collective-permute-done
  63.2 6.3 collective-permute-done
  74.6 6.3 collective-permute-done
  86.0 6.3 collective-permute-done
  97.4 6.3 collective-permute-done
  108.8 6.8 %collective-permute-done = bf16[256,128]{1,0:T(8,128)(2,1)S(1)} collective-permute-done((bf16[256,128]{1,0:T(8,128)(2,1)S(1)}, bf16[256,128]{1,0:T(8,128)(2,1)S(1)}, u32[]{:S(2)}, u32[]{:S(2)}) %collective-permute-start) | collective-permute-done | bytes 65568 | tf_op jit(solution)/shard_map/while/body/eval_jaxpr/ppermute | solution.py:16
  120.7 6.3 collective-permute-done
  132.1 6.3 collective-permute-done
  143.5 6.3 collective-permute-done
  154.8 6.3 collective-permute-done
  166.2 6.3 collective-permute-done
  177.6 6.3 collective-permute-done
  193.0 77.2 %reduce-scatter.2.cloned.1.call-done = f32[256,128]{1,0:T(8,128)} async-done(((f32[4096,128]{1,0:T(8,128)}), f32[256,128]{1,0:T(8,128)}) %reduce-scatter.2.cloned.1.call-update) | async-done | bytes 131088 | tf_op jit(solution)/shard_map/reduce_scatter | solution.py:62
  273.4 5.5 all-to-all-start
  280.9 80.1 %psum.23 = f32[256]{0:T(256)} all-reduce(f32[256]{0:T(256)S(1)} %broadcast_multiply_fusion), channel_id=1, replica_groups=mesh['loop'=16,'rep'=16] {'loop','rep'}, use_global_device_ids=true, to_apply=%region_8.11 | all-reduce | flops 256 | bytes 2048 | tf_op jit(solution)/shard_map/psum | solution.py:83
  361.0 177.1 %all-reduce.3.cloned.1.call-done = (f32[128,256]{0,1:T(8,128)}, f32[128,256]{1,0:T(8,128)}) async-done(((f32[128,256]{0,1:T(8,128)}, f32[128,256]{1,0:T(8,128)}), (f32[128,256]{0,1:T(8,128)}, f32[128,256]{1,0:T(8,128)})) %all-reduce.3.cloned.1.call-update) | async-done | bytes 262160 | tf_op jit(solution)/shard_map/psum | solution.py:83
  542.9 111.3 %while.33 = (s32[]{:T(128)}, f32[256,128]{1,0:T(8,128)S(1)}, s32[]{:T(128)}, f32[16,16,2]{1,2,0:T(2,128)S(1)}, bf16[16,16,128,128]{3,2,1,0:T(8,128)(2,1)}, /*ind...) while((s32[]{:T(128)}, f32[256,128]{1,0:T(8,128)S(1)}, ...), condition=%wide.region_4.7_spmd, body=%wide.region_3.6_spmd.sunk | while | flops 73696368 | bytes 5510748 | solution.py:108
  548.3 4.2 collective-permute-start.1
  556.6 3.7 collective-permute-start.1
  564.4 3.1 collective-permute-start.1
  578.7 3.1 collective-permute-start.1
  585.9 3.6 collective-permute-start.1
  593.6 4.3 collective-permute-start.1
  601.9 3.5 collective-permute-start.1
  609.5 3.1 collective-permute-start.1
  631.0 4.0 collective-permute-start.1
  639.0 4.0 collective-permute-start.1
  647.1 3.1 collective-permute-start.1
  (279 shorter events, 170.2 us)
Async XLA Ops:
  7.2 262.9 %reduce-scatter.2.cloned.1.call-start = ((), (), s32[]{:S(2)}) async-start(), calls=%async_computation.2 | async-start | bytes 2228224 | tf_op jit(solution)/shard_map/reduce_scatter | solution.py:62
  14.8 9.2 %collective-permute-start = (bf16[256,128]{1,0:T(8,128)(2,1)S(1)}, bf16[256,128]{1,0:T(8,128)(2,1)S(1)}, u32[]{:S(2)}, u32[]{:S(2)}) collective-permute-start(bf16[256,128]{1,0:T(8,128)(2,1)S(1)} %get-tuple-element.526), channel_id=1, source_target_pairs={{240,0},{0,16},{16,32},{32,48},{48,64},{64,80},{80,96},{96,112},{1... | collective-permute-start | bytes 196616 | tf_op jit(solution)/shard_map/while/body/eval_jaxpr/ppermute | solution.py:16
  28.9 6.5 collective-permute-start
  40.3 6.5 collective-permute-start
  51.7 6.5 collective-permute-start
  63.1 6.5 collective-permute-start
  74.5 6.5 collective-permute-start
  85.9 6.5 collective-permute-start
  97.3 6.5 collective-permute-start
  108.6 7.0 %collective-permute-start = (bf16[256,128]{1,0:T(8,128)(2,1)S(1)}, bf16[256,128]{1,0:T(8,128)(2,1)S(1)}, u32[]{:S(2)}, u32[]{:S(2)}) collective-permute-start(bf16[256,128]{1,0:T(8,128)(2,1)S(1)} %get-tuple-element.526), channel_id=1, source_target_pairs={{240,0},{0,16},{16,32},{32,48},{48,64},{64,80},{80,96},{96,112},{1... | collective-permute-start | bytes 196616 | tf_op jit(solution)/shard_map/while/body/eval_jaxpr/ppermute | solution.py:16
  120.5 6.5 collective-permute-start
  131.9 6.5 collective-permute-start
  143.3 6.5 collective-permute-start
  154.7 6.5 collective-permute-start
  166.1 6.5 collective-permute-start
  177.5 6.5 collective-permute-start
  273.4 266.3 %all-to-all-start = ((bf16[16,256,128]{2,1,0:T(8,128)(2,1)}), bf16[16,256,128]{2,1,0:T(8,128)(2,1)S(1)}, u32[]{:S(2)}, u32[]{:S(2)}) async-start(bf16[16,256,128]{2,1,0:T(8,128)(2,1)} %stack.2), calls=%async_computation.1 | async-start | bytes 2097152 | tf_op jit(solution)/shard_map/all_to_all | solution.py:10
  278.9 259.2 %all-reduce.3.cloned.1.call-start = ((), (), s32[]{:S(2)}) async-start(), calls=%async_computation.3 | async-start | bytes 524288 | tf_op jit(solution)/shard_map/psum | solution.py:83
  548.3 8.2 %collective-permute-start.1 = (f32[256,128]{1,0:T(8,128)S(1)}, f32[256,128]{1,0:T(8,128)S(1)}, u32[]{:S(2)}, u32[]{:S(2)}) collective-permute-start(f32[256,128]{1,0:T(8,128)S(1)} %get-tuple-element.559), channel_id=1, source_target_pairs={{16,0},{32,16},{48,32},{64,48},{80,64},{96,80},{112,96},{128,112},... | collective-permute-start | bytes 393224 | tf_op jit(solution)/shard_map/while/body/eval_jaxpr/ppermute | solution.py:16
  556.6 7.7 %collective-permute-start.1 = (f32[256,128]{1,0:T(8,128)S(1)}, f32[256,128]{1,0:T(8,128)S(1)}, u32[]{:S(2)}, u32[]{:S(2)}) collective-permute-start(f32[256,128]{1,0:T(8,128)S(1)} %get-tuple-element.559), channel_id=1, source_target_pairs={{16,0},{32,16},{48,32},{64,48},{80,64},{96,80},{112,96},{128,112},... | collective-permute-start | bytes 393224 | tf_op jit(solution)/shard_map/while/body/eval_jaxpr/ppermute | solution.py:16
  564.4 7.1 %collective-permute-start.1 = (f32[256,128]{1,0:T(8,128)S(1)}, f32[256,128]{1,0:T(8,128)S(1)}, u32[]{:S(2)}, u32[]{:S(2)}) collective-permute-start(f32[256,128]{1,0:T(8,128)S(1)} %get-tuple-element.559), channel_id=1, source_target_pairs={{16,0},{32,16},{48,32},{64,48},{80,64},{96,80},{112,96},{128,112},... | collective-permute-start | bytes 393224 | tf_op jit(solution)/shard_map/while/body/eval_jaxpr/ppermute | solution.py:16
  571.5 7.1 %collective-permute-start.1 = (f32[256,128]{1,0:T(8,128)S(1)}, f32[256,128]{1,0:T(8,128)S(1)}, u32[]{:S(2)}, u32[]{:S(2)}) collective-permute-start(f32[256,128]{1,0:T(8,128)S(1)} %get-tuple-element.559), channel_id=1, source_target_pairs={{16,0},{32,16},{48,32},{64,48},{80,64},{96,80},{112,96},{128,112},... | collective-permute-start | bytes 393224 | tf_op jit(solution)/shard_map/while/body/eval_jaxpr/ppermute | solution.py:16
  578.7 7.1 %collective-permute-start.1 = (f32[256,128]{1,0:T(8,128)S(1)}, f32[256,128]{1,0:T(8,128)S(1)}, u32[]{:S(2)}, u32[]{:S(2)}) collective-permute-start(f32[256,128]{1,0:T(8,128)S(1)} %get-tuple-element.559), channel_id=1, source_target_pairs={{16,0},{32,16},{48,32},{64,48},{80,64},{96,80},{112,96},{128,112},... | collective-permute-start | bytes 393224 | tf_op jit(solution)/shard_map/while/body/eval_jaxpr/ppermute | solution.py:16
  585.9 7.6 %collective-permute-start.1 = (f32[256,128]{1,0:T(8,128)S(1)}, f32[256,128]{1,0:T(8,128)S(1)}, u32[]{:S(2)}, u32[]{:S(2)}) collective-permute-start(f32[256,128]{1,0:T(8,128)S(1)} %get-tuple-element.559), channel_id=1, source_target_pairs={{16,0},{32,16},{48,32},{64,48},{80,64},{96,80},{112,96},{128,112},... | collective-permute-start | bytes 393224 | tf_op jit(solution)/shard_map/while/body/eval_jaxpr/ppermute | solution.py:16
  593.6 8.3 %collective-permute-start.1 = (f32[256,128]{1,0:T(8,128)S(1)}, f32[256,128]{1,0:T(8,128)S(1)}, u32[]{:S(2)}, u32[]{:S(2)}) collective-permute-start(f32[256,128]{1,0:T(8,128)S(1)} %get-tuple-element.559), channel_id=1, source_target_pairs={{16,0},{32,16},{48,32},{64,48},{80,64},{96,80},{112,96},{128,112},... | collective-permute-start | bytes 393224 | tf_op jit(solution)/shard_map/while/body/eval_jaxpr/ppermute | solution.py:16
  601.9 7.5 %collective-permute-start.1 = (f32[256,128]{1,0:T(8,128)S(1)}, f32[256,128]{1,0:T(8,128)S(1)}, u32[]{:S(2)}, u32[]{:S(2)}) collective-permute-start(f32[256,128]{1,0:T(8,128)S(1)} %get-tuple-element.559), channel_id=1, source_target_pairs={{16,0},{32,16},{48,32},{64,48},{80,64},{96,80},{112,96},{128,112},... | collective-permute-start | bytes 393224 | tf_op jit(solution)/shard_map/while/body/eval_jaxpr/ppermute | solution.py:16
  609.5 7.1 %collective-permute-start.1 = (f32[256,128]{1,0:T(8,128)S(1)}, f32[256,128]{1,0:T(8,128)S(1)}, u32[]{:S(2)}, u32[]{:S(2)}) collective-permute-start(f32[256,128]{1,0:T(8,128)S(1)} %get-tuple-element.559), channel_id=1, source_target_pairs={{16,0},{32,16},{48,32},{64,48},{80,64},{96,80},{112,96},{128,112},... | collective-permute-start | bytes 393224 | tf_op jit(solution)/shard_map/while/body/eval_jaxpr/ppermute | solution.py:16
  616.6 7.1 %collective-permute-start.1 = (f32[256,128]{1,0:T(8,128)S(1)}, f32[256,128]{1,0:T(8,128)S(1)}, u32[]{:S(2)}, u32[]{:S(2)}) collective-permute-start(f32[256,128]{1,0:T(8,128)S(1)} %get-tuple-element.559), channel_id=1, source_target_pairs={{16,0},{32,16},{48,32},{64,48},{80,64},{96,80},{112,96},{128,112},... | collective-permute-start | bytes 393224 | tf_op jit(solution)/shard_map/while/body/eval_jaxpr/ppermute | solution.py:16
  623.8 7.1 %collective-permute-start.1 = (f32[256,128]{1,0:T(8,128)S(1)}, f32[256,128]{1,0:T(8,128)S(1)}, u32[]{:S(2)}, u32[]{:S(2)}) collective-permute-start(f32[256,128]{1,0:T(8,128)S(1)} %get-tuple-element.559), channel_id=1, source_target_pairs={{16,0},{32,16},{48,32},{64,48},{80,64},{96,80},{112,96},{128,112},... | collective-permute-start | bytes 393224 | tf_op jit(solution)/shard_map/while/body/eval_jaxpr/ppermute | solution.py:16
  631.0 8.0 %collective-permute-start.1 = (f32[256,128]{1,0:T(8,128)S(1)}, f32[256,128]{1,0:T(8,128)S(1)}, u32[]{:S(2)}, u32[]{:S(2)}) collective-permute-start(f32[256,128]{1,0:T(8,128)S(1)} %get-tuple-element.559), channel_id=1, source_target_pairs={{16,0},{32,16},{48,32},{64,48},{80,64},{96,80},{112,96},{128,112},... | collective-permute-start | bytes 393224 | tf_op jit(solution)/shard_map/while/body/eval_jaxpr/ppermute | solution.py:16
  639.0 8.0 %collective-permute-start.1 = (f32[256,128]{1,0:T(8,128)S(1)}, f32[256,128]{1,0:T(8,128)S(1)}, u32[]{:S(2)}, u32[]{:S(2)}) collective-permute-start(f32[256,128]{1,0:T(8,128)S(1)} %get-tuple-element.559), channel_id=1, source_target_pairs={{16,0},{32,16},{48,32},{64,48},{80,64},{96,80},{112,96},{128,112},... | collective-permute-start | bytes 393224 | tf_op jit(solution)/shard_map/while/body/eval_jaxpr/ppermute | solution.py:16
  647.1 7.1 %collective-permute-start.1 = (f32[256,128]{1,0:T(8,128)S(1)}, f32[256,128]{1,0:T(8,128)S(1)}, u32[]{:S(2)}, u32[]{:S(2)}) collective-permute-start(f32[256,128]{1,0:T(8,128)S(1)} %get-tuple-element.559), channel_id=1, source_target_pairs={{16,0},{32,16},{48,32},{64,48},{80,64},{96,80},{112,96},{128,112},... | collective-permute-start | bytes 393224 | tf_op jit(solution)/shard_map/while/body/eval_jaxpr/ppermute | solution.py:16
  (10 other events, 550.7 us)
Sparse Core Ops, SparseCore 0:
  191.6 78.5 reduce-scatter.1
  285.9 252.1 all-reduce.2
